TPU v7x, 256 devices: a whole 4x4x8 slice. The times are simulated.
256 devices in a mesh: seq: 64 (over y, z_hi, x, core), dp: 4 (over z_lo).
Axes of the slice: x: 4, y: 4, z: 8 (z_hi: 2, z_lo: 4; z = z_hi * 4 + z_lo), core: 2. Of those that a mesh axis runs over, the one named last changes fastest.
Arguments:
- inputs: bfloat16 [4, 64, 512, 512], P('dp', 'seq'), may hold values from -16 to 16
- norm_gain: float32 [512], replicated, may hold values from 0.25 to 1.75
- qkv_weight: bfloat16 [512, 1536], replicated, may hold values from -2 to 2
- out_weight: bfloat16 [512, 512], replicated, may hold values from -0.25 to 0.25
- out_cotan: bfloat16 [4, 64, 512, 512], P('dp', 'seq'), may hold values from -6 to 6
Outputs:
- input_grad: bfloat16 [4, 64, 512, 512], P('dp', 'seq')
- qkv_weight_grad: float32 [512, 1536], P('seq')
- out_weight_grad: float32 [512, 512], P('seq')
- gain_grad: float32 [512], P('seq')
All inputs are finite; a program needn't handle non-finite values.
Results may differ from a plain program's by a relative error of at most 0.0091.
Values may be sent and summed in bfloat16 or wider, within the bound.
A program may use at most 64 MiB of HBM per device.

v0:
```python
import math
import jax
import jax.numpy as jnp
from jax import lax
from jax.sharding import PartitionSpec as P

H = 8
HD = 64


def blocked(kernel, arrays, group_size):
    block_count = arrays[0].shape[0] // group_size
    split_arrays = tuple(
        (member.reshape((block_count, group_size) + member.shape[1:]) for member in arrays)
    )
    result = lax.map(lambda pieces: kernel(*pieces), split_arrays)
    return jax.tree.map(
        lambda member: member.reshape((block_count * group_size,) + member.shape[2:]), result
    )


def attend_probs(queries, key_vals):
    score_scale = HD ** (-0.5)
    scores = (
        jnp.einsum("glhd,gmhd->ghlm", queries, key_vals, preferred_element_type=jnp.float32)
        * score_scale
    )
    length = queries.shape[1]
    causal = lax.broadcasted_iota(jnp.int32, (length, length), 0) >= lax.broadcasted_iota(
        jnp.int32, (length, length), 1
    )
    scores = jnp.where(causal, scores, -1e30)
    row_max = jnp.max(scores, -1, keepdims=True)
    exponent = jnp.exp(scores - row_max)
    return exponent / jnp.sum(exponent, -1, keepdims=True)


def forward_block(queries, key_vals, values):
    weights = attend_probs(queries, key_vals).astype(jnp.bfloat16)
    return jnp.einsum(
        "ghlm,gmhd->glhd", weights, values, preferred_element_type=jnp.float32
    ).astype(jnp.bfloat16)


def backward_block(queries, key_vals, values, attended, cotangent):
    score_scale = HD ** (-0.5)
    softmax_probs = attend_probs(queries, key_vals)
    weights = softmax_probs.astype(jnp.bfloat16)
    prob_grad = jnp.einsum("glhd,gmhd->ghlm", cotangent, values, preferred_element_type=jnp.float32)
    row_delta = jnp.sum(cotangent.astype(jnp.float32) * attended.astype(jnp.float32), -1)
    row_delta = jnp.transpose(row_delta, (0, 2, 1))[..., None]
    score_grad = (softmax_probs * (prob_grad - row_delta)).astype(jnp.bfloat16)
    grad_query = (
        jnp.einsum("ghlm,gmhd->glhd", score_grad, key_vals, preferred_element_type=jnp.float32)
        * score_scale
    ).astype(jnp.bfloat16)
    grad_keys = (
        jnp.einsum("ghlm,glhd->gmhd", score_grad, queries, preferred_element_type=jnp.float32)
        * score_scale
    ).astype(jnp.bfloat16)
    grad_values = jnp.einsum(
        "ghlm,glhd->gmhd", weights, cotangent, preferred_element_type=jnp.float32
    ).astype(jnp.bfloat16)
    return (grad_query, grad_keys, grad_values)


def body(inputs, norm_gain, qkv_weight, out_weight, out_cotan):
    band_rows = inputs.shape[1]
    columns = inputs.shape[2]
    feature_width = inputs.shape[3]
    seq_count = lax.axis_size("seq")
    all_rows = band_rows * seq_count
    col_share = columns // seq_count
    half_heads = H // 2
    half_width = half_heads * HD
    tokens = band_rows * columns
    flat_input = inputs.reshape(tokens, feature_width).astype(jnp.float32)
    inverse_rms = lax.rsqrt(jnp.mean(flat_input * flat_input, -1, keepdims=True) + 1e-05)
    normed = flat_input * inverse_rms
    hidden = (normed * norm_gain).astype(jnp.bfloat16)
    weight_parts = qkv_weight.reshape(feature_width, 3, H, HD)
    weight_rows = weight_parts[:, :, :half_heads].reshape(feature_width, 3 * half_width)
    weight_cols = weight_parts[:, :, half_heads:].reshape(feature_width, 3 * half_width)
    row_proj = jnp.dot(hidden, weight_rows, preferred_element_type=jnp.float32).astype(jnp.bfloat16)
    row_grid = row_proj.reshape(band_rows, columns, 3, half_heads, HD)
    flat_cotan = out_cotan.reshape(tokens, feature_width)
    grad_att = jnp.dot(flat_cotan, out_weight.T, preferred_element_type=jnp.float32).astype(
        jnp.bfloat16
    )
    att_cot_grid = grad_att.reshape(band_rows, columns, H, HD)
    col_cot = att_cot_grid[:, :, half_heads:].reshape(band_rows, columns, half_width)
    col_group = math.gcd(col_share, max(1, 512 // all_rows))
    col_qkv = (
        jnp.dot(hidden, weight_cols, preferred_element_type=jnp.float32)
        .astype(jnp.bfloat16)
        .reshape(band_rows, columns, 3 * half_width)
    )
    received = lax.all_to_all(col_qkv, "seq", split_axis=1, concat_axis=0, tiled=True)
    col_grid = jnp.swapaxes(received, 0, 1).reshape(col_share, all_rows, 3, half_heads, HD)
    cols_in = (col_grid[:, :, 0], col_grid[:, :, 1], col_grid[:, :, 2])
    col_att = blocked(forward_block, cols_in, col_group)
    sent_att = jnp.swapaxes(col_att, 0, 1).reshape(all_rows, col_share, half_width)
    col_out = lax.all_to_all(sent_att, "seq", split_axis=0, concat_axis=1, tiled=True)
    received_cot = lax.all_to_all(col_cot, "seq", split_axis=1, concat_axis=0, tiled=True)
    cot_grid = jnp.swapaxes(received_cot, 0, 1).reshape(col_share, all_rows, half_heads, HD)
    col_grads = blocked(backward_block, cols_in + (col_att, cot_grid), col_group)
    stacked = jnp.swapaxes(jnp.stack(col_grads, 2), 0, 1).reshape(
        all_rows, col_share, 3 * half_width
    )
    col_dqkv = lax.all_to_all(stacked, "seq", split_axis=0, concat_axis=1, tiled=True)
    row_group = math.gcd(band_rows, max(1, 512 // columns))
    rows_in = (row_grid[:, :, 0], row_grid[:, :, 1], row_grid[:, :, 2])
    row_att = blocked(forward_block, rows_in, row_group)
    row_grads = blocked(
        backward_block, rows_in + (row_att, att_cot_grid[:, :, :half_heads]), row_group
    )
    attended = jnp.concatenate(
        [row_att, col_out.reshape(band_rows, columns, half_heads, HD)], 2
    ).reshape(tokens, feature_width)
    row_dqkv = jnp.stack(row_grads, 2)
    grad_qkv = jnp.concatenate(
        [row_dqkv, col_dqkv.reshape(band_rows, columns, 3, half_heads, HD)], 3
    ).reshape(tokens, 3 * feature_width)
    term_out = jnp.dot(attended.T, flat_cotan, preferred_element_type=jnp.float32)
    term_qkv = jnp.dot(hidden.T, grad_qkv, preferred_element_type=jnp.float32)
    grad_hidden = jnp.dot(grad_qkv, qkv_weight.T, preferred_element_type=jnp.float32)
    term_gain = jnp.sum(grad_hidden * normed, 0)
    grad_normed = grad_hidden * norm_gain
    grad_input = inverse_rms * (
        grad_normed - normed * jnp.mean(grad_normed * normed, -1, keepdims=True)
    )
    input_grad = (
        (flat_cotan.astype(jnp.float32) + grad_input).astype(jnp.bfloat16).reshape(inputs.shape)
    )
    full_qkv, full_out, full_gain = lax.psum((term_qkv, term_out, term_gain), ("seq", "dp"))
    row_share = feature_width // seq_count
    first_row = lax.axis_index("seq") * row_share
    sum_qkv = lax.dynamic_slice_in_dim(full_qkv, first_row, row_share, 0)
    sum_out = lax.dynamic_slice_in_dim(full_out, first_row, row_share, 0)
    sum_gain = lax.dynamic_slice_in_dim(full_gain, first_row, row_share, 0)
    return (input_grad, sum_qkv, sum_out, sum_gain)


def solution(mesh):
    return jax.shard_map(
        body,
        mesh=mesh,
        in_specs=(P("dp", "seq", None, None), P(), P(), P(), P("dp", "seq", None, None)),
        out_specs=(P("dp", "seq", None, None), P("seq", None), P("seq", None), P("seq")),
        check_vma=False,
    )
```

profile of v0, /device:TPU:97, one launch (start us, length us, event | category | flops | bytes accessed | tf_op | source)
XLA Modules:
  0.0 445.4 jit_solution(2909566753671628092)
XLA Ops:
  11.5 2.2 reduce.5
  14.6 12.3 %all-to-all-start.1 = ((bf16[64,2,1024]{2,1,0:T(2,128)(2,1)}), bf16[64,2,1024]{2,1,0:T(2,128)(2,1)}, u32[]{:S(2)}, u32[]{:S(2)}) async-start(bf16[64,2,1024]{2,1,0:T(2,128)(2,1)} %reshape.245), calls=%async_computation.1 | async-start | bytes 524288 | tf_op jit(solution)/shard_map/all_to_all | solution.py:104
  31.7 5.4 %reduce.6 = bf16[512,768]{1,0:T(8,128)(2,1)S(1)} reduce(bf16[512,1,768]{2,1,0:T(2,128)(2,1)S(1)} %bitcast.188, bf16[]{:T(256)} %broadcast.106), dimensions={1}, to_apply=%bitcast.186.reduce_sub_computation | reduce | bytes 1572866
  38.3 2.2 all-to-all-done.1
  40.5 10.7 %all-to-all-start = ((bf16[64,2,3072]{2,1,0:T(2,128)(2,1)}), bf16[64,2,3072]{2,1,0:T(2,128)(2,1)}, u32[]{:S(2)}, u32[]{:S(2)}) async-start(bf16[64,2,3072]{2,1,0:T(2,128)(2,1)} %reshape.247), calls=%async_computation | async-start | bytes 1572864 | tf_op jit(solution)/shard_map/all_to_all | solution.py:98
  52.3 3.6 fusion.63
  55.9 2.8 fusion.6
  58.8 2.1 multiply_reduce_fusion
  60.9 2.8 reshape.246
  65.8 7.4 %all-to-all-done = bf16[64,2,3072]{2,1,0:T(2,128)(2,1)} async-done(((bf16[64,2,3072]{2,1,0:T(2,128)(2,1)}), bf16[64,2,3072]{2,1,0:T(2,128)(2,1)}, u32[]{:S(2)}, u32[]{:S(2)}) %all-to-all-start) | async-done | bytes 786464 | tf_op jit(solution)/shard_map/all_to_all | solution.py:98
  73.2 5.8 %reshape.248 = bf16[512,1,768]{2,1,0:T(2,128)(2,1)} reshape(bf16[64,2,3072]{2,1,0:T(2,128)(2,1)} %all-to-all-done) | data formatting | bytes 1572864
  79.0 2.4 copy.166
  81.4 3.5 reshape.243
  84.9 2.7 fusion.61
  89.4 3.3 fusion.38
  92.7 2.0 copy.141
  94.7 7.6 %all-to-all-start.3 = ((bf16[64,8,256]{2,1,0:T(8,128)(2,1)}), bf16[64,8,256]{2,1,0:T(8,128)(2,1)S(1)}, u32[]{:S(2)}, u32[]{:S(2)}) async-start(bf16[64,8,256]{2,1,0:T(8,128)(2,1)} %copy.141), calls=%async_computation.3 | async-start | bytes 524288 | tf_op jit(solution)/shard_map/all_to_all | solution.py:103
  102.3 2.8 fusion.16
  105.0 3.0 fusion.22
  111.6 2.4 copy.121
  114.0 3.6 reshape.235
  117.6 12.9 %all-to-all-start.2 = ((bf16[64,8,768]{2,1,0:T(8,128)(2,1)}), bf16[64,8,768]{2,1,0:T(8,128)(2,1)}, u32[]{:S(2)}, u32[]{:S(2)}) async-start(bf16[64,8,768]{2,1,0:T(8,128)(2,1)} %reshape.235), calls=%async_computation.2 | async-start | bytes 1572864 | tf_op jit(solution)/shard_map/all_to_all | solution.py:110
  130.6 1.8 fusion.28
  132.4 2.9 multiply_convert_fusion
  140.1 13.3 %all-to-all-done.2 = bf16[64,8,768]{2,1,0:T(8,128)(2,1)} async-done(((bf16[64,8,768]{2,1,0:T(8,128)(2,1)}), bf16[64,8,768]{2,1,0:T(8,128)(2,1)}, u32[]{:S(2)}, u32[]{:S(2)}) %all-to-all-start.2) | async-done | bytes 786464 | tf_op jit(solution)/shard_map/all_to_all | solution.py:110
  153.4 2.8 reshape.236
  156.1 2.3 copy.122
  159.9 2.9 fusion.54
  162.8 3.6 fusion.34
  166.4 78.7 %psum.23 = f32[512]{0:T(512)S(1)} all-reduce(f32[512]{0:T(512)S(1)} %get-tuple-element.60), channel_id=1, replica_groups=mesh['seq'=64,'dp'=4] {'seq','dp'}, use_global_device_ids=true, to_apply=%region_11.12 | all-reduce | flops 512 | bytes 4096 | tf_op jit(solution)/shard_map/psum | solution.py:135
  245.7 2.4 fusion.40
  248.0 187.8 %all-reduce.3.cloned.1.call-done = (f32[512,1536]{1,0:T(8,128)}, f32[512,512]{1,0:T(8,128)}) async-done(((f32[512,1536]{1,0:T(8,128)}, f32[512,512]{1,0:T(8,128)}), (f32[512,1536]{1,0:T(8,128)}, f32[512,512]{1,0:T(8,128)})) %all-reduce.3.cloned.1.call-update) | async-done | bytes 4194320 | tf_op jit(solution)/shard_map/psum | solution.py:135
  (71 shorter events, 29.1 us)
Async XLA Ops:
  7.2 1.0 copy-start
  7.2 19.7 %copy-start.1 = (bf16[1,1,512,512]{3,2,1,0:T(8,128)(2,1)S(1)}, bf16[1,1,512,512]{3,2,1,0:T(8,128)(2,1)}, u32[]{:S(2)}) copy-start(bf16[1,1,512,512]{3,2,1,0:T(8,128)(2,1)} %param.5) | copy-start | bytes 1572868
  9.7 0.8 copy-start.3
  14.6 26.0 %all-to-all-start.1 = ((bf16[64,2,1024]{2,1,0:T(2,128)(2,1)}), bf16[64,2,1024]{2,1,0:T(2,128)(2,1)}, u32[]{:S(2)}, u32[]{:S(2)}) async-start(bf16[64,2,1024]{2,1,0:T(2,128)(2,1)} %reshape.245), calls=%async_computation.1 | async-start | bytes 524288 | tf_op jit(solution)/shard_map/all_to_all | solution.py:104
  28.8 1.0 copy-start.16
  37.1 14.1 %copy-start.14 = (bf16[512,3,4,64]{0,3,2,1:T(8,128)(2,1)S(1)}, bf16[512,3,4,64]{0,3,2,1:T(8,128)(2,1)}, u32[]{:S(2)}) copy-start(bf16[512,3,4,64]{0,3,2,1:T(8,128)(2,1)} %get-tuple-element.69) | copy-start | bytes 2359300
  40.5 32.7 %all-to-all-start = ((bf16[64,2,3072]{2,1,0:T(2,128)(2,1)}), bf16[64,2,3072]{2,1,0:T(2,128)(2,1)}, u32[]{:S(2)}, u32[]{:S(2)}) async-start(bf16[64,2,3072]{2,1,0:T(2,128)(2,1)} %reshape.247), calls=%async_computation | async-start | bytes 1572864 | tf_op jit(solution)/shard_map/all_to_all | solution.py:98
  52.2 3.7 copy-start.6
  55.9 2.8 copy-start.4
  87.6 1.8 copy-start.8
  87.6 1.8 copy-start.9
  88.1 1.3 copy-start.12
  94.7 22.9 %all-to-all-start.3 = ((bf16[64,8,256]{2,1,0:T(8,128)(2,1)}), bf16[64,8,256]{2,1,0:T(8,128)(2,1)S(1)}, u32[]{:S(2)}, u32[]{:S(2)}) async-start(bf16[64,8,256]{2,1,0:T(8,128)(2,1)} %copy.141), calls=%async_computation.3 | async-start | bytes 524288 | tf_op jit(solution)/shard_map/all_to_all | solution.py:103
  108.0 3.2 copy-start.15
  117.6 12.9 %copy-start.10 = (bf16[64,8,256]{2,1,0:T(8,128)(2,1)}, bf16[64,8,256]{2,1,0:T(8,128)(2,1)S(1)}, u32[]{:S(2)}) copy-start(bf16[64,8,256]{2,1,0:T(8,128)(2,1)S(1)} %all-to-all-done.3) | copy-start | bytes 786436
  117.6 35.8 %all-to-all-start.2 = ((bf16[64,8,768]{2,1,0:T(8,128)(2,1)}), bf16[64,8,768]{2,1,0:T(8,128)(2,1)}, u32[]{:S(2)}, u32[]{:S(2)}) async-start(bf16[64,8,768]{2,1,0:T(8,128)(2,1)} %reshape.235), calls=%async_computation.2 | async-start | bytes 1572864 | tf_op jit(solution)/shard_map/all_to_all | solution.py:110
  130.5 305.3 %all-reduce.3.cloned.1.call-start = ((), (), s32[]{:S(2)}) async-start(), calls=%async_computation.4 | async-start | bytes 8388608 | tf_op jit(solution)/shard_map/psum | solution.py:135
  130.6 1.8 copy-start.5
  130.6 1.8 copy-start.7
  135.4 2.7 copy-start.11
  136.8 1.8 copy-start.13
  136.8 1.8 copy-start.2
Sparse Core Ops, SparseCore 0:
  162.9 272.8 all-reduce.2
where the time goes:
time: 447 us; the launch traced here: 445 us
  waiting for transfers between devices  211 us (47%)
  blocking collectives  78.7 us (18%)
  local copies, waits for them, and re-layouts  45.3 us (10%)
  starting transfers between devices  43.5 us (10%)
  matrix products  36.5 us (8%)
  other arithmetic  16.3 us (4%)
  between operations  14.4 us (3%)
    psum x1, waiting for transfers between devices, body(): lax.psum((term_qkv, term_out, term_gain), ('seq', 'dp'))  188 us
    psum x1, blocking collectives, body(): lax.psum((term_qkv, term_out, term_gain), ('seq', 'dp'))  78.7 us
    unnamed x42, local copies, waits for them, and re-layouts  18.2 us
    all_to_all x1, waiting for transfers between devices, body(): lax.all_to_all(stacked, 'seq', split_axis=0, concat_axis=1, tiled=True)  13.3 us
    all_to_all x1, starting transfers between devices, body(): lax.all_to_all(stacked, 'seq', split_axis=0, concat_axis=1, tiled=True)  12.9 us
    all_to_all x1, starting transfers between devices, body(): lax.all_to_all(col_cot, 'seq', split_axis=1, concat_axis=0, tiled=True)  12.3 us
    all_to_all x1, starting transfers between devices, body(): lax.all_to_all(col_qkv, 'seq', split_axis=1, concat_axis=0, tiled=True)  10.7 us
  transfers between devices with their start and end apart: 5, of which 4 were waited for; matrix products, arithmetic and copies ran while one was open for 13% of the time, Pallas kernels for 0%

commit v1 on v0

--- a/solution.py
+++ b/solution.py
@@ -6,6 +6,11 @@
 
 H = 8
 HD = 64
+
+
+def axis_by_axis(array, first, second):
+    half = lax.psum(array, first)
+    return lax.psum(half, second)
 
 
 def blocked(kernel, arrays, group_size):
@@ -132,7 +137,7 @@
     input_grad = (
         (flat_cotan.astype(jnp.float32) + grad_input).astype(jnp.bfloat16).reshape(inputs.shape)
     )
-    full_qkv, full_out, full_gain = lax.psum((term_qkv, term_out, term_gain), ("seq", "dp"))
+    full_qkv, full_out, full_gain = axis_by_axis((term_qkv, term_out, term_gain), "seq", "dp")
     row_share = feature_width // seq_count
     first_row = lax.axis_index("seq") * row_share
     sum_qkv = lax.dynamic_slice_in_dim(full_qkv, first_row, row_share, 0)

time: 447 us -> 1240 us (2.77); the launches traced: 445 us -> 1220 us
  waiting for transfers between devices: 211 us -> 820 us
  blocking collectives: 78.7 us -> 245 us
    psum x1 -> x2, waiting for transfers between devices: 188 us -> 797 us  [the longest x1 797 us: axis_by_axis(): half = lax.psum(array, first)]
    psum x1 -> x2, blocking collectives: 78.7 us -> 245 us  [the longest x1 209 us: axis_by_axis(): half = lax.psum(array, first)]
  transfers between devices with their start and end apart: 5 -> 6, of which waited for: 4 -> 4; matrix products, arithmetic and copies ran while one was open for 13% -> 5% of each run, Pallas kernels for 0% -> 0%
where the time goes in v1:
time: 1240 us; the launch traced here: 1220 us
  waiting for transfers between devices  820 us (66%)
  blocking collectives  245 us (20%)
  local copies, waits for them, and re-layouts  45.3 us (4%)
  starting transfers between devices  43.6 us (4%)
  matrix products  36.5 us (3%)
  other arithmetic  16.3 us (1%)
  between operations  14.4 us (1%)
    psum x1, waiting for transfers between devices, axis_by_axis(): half = lax.psum(array, first)  797 us
    psum x1, blocking collectives, axis_by_axis(): half = lax.psum(array, first)  209 us
    psum x1, blocking collectives, axis_by_axis(): return lax.psum(half, second)  36.5 us
  transfers between devices with their start and end apart: 6, of which 4 were waited for; matrix products, arithmetic and copies ran while one was open for 5% of the time, Pallas kernels for 0%

profile of v1, /device:TPU:97, one launch (start us, length us, event | category | flops | bytes accessed | tf_op | source)
XLA Modules:
  0.0 1221.5 jit_solution(8506878034471749433)
XLA Ops:
  11.5 2.2 reduce.5
  14.6 12.3 %all-to-all-start.1 = ((bf16[64,2,1024]{2,1,0:T(2,128)(2,1)}), bf16[64,2,1024]{2,1,0:T(2,128)(2,1)}, u32[]{:S(2)}, u32[]{:S(2)}) async-start(bf16[64,2,1024]{2,1,0:T(2,128)(2,1)} %reshape.245), calls=%async_computation.1 | async-start | bytes 524288 | tf_op jit(solution)/shard_map/all_to_all | solution.py:109
  31.7 5.4 reduce.6
  38.3 2.2 all-to-all-done.1
  40.5 10.7 all-to-all-start
  52.3 3.6 fusion.63
  55.9 2.8 fusion.6
  58.8 2.1 multiply_reduce_fusion
  60.9 2.8 reshape.246
  65.8 7.4 all-to-all-done
  73.2 5.8 reshape.248
  79.0 2.4 copy.166
  81.4 3.5 reshape.243
  84.9 2.7 fusion.61
  89.4 3.3 fusion.38
  92.7 2.0 copy.141
  94.7 7.6 all-to-all-start.3
  102.3 2.8 fusion.16
  105.0 3.0 fusion.22
  111.6 2.4 copy.121
  114.0 3.6 reshape.235
  117.6 12.9 %all-to-all-start.2 = ((bf16[64,8,768]{2,1,0:T(8,128)(2,1)}), bf16[64,8,768]{2,1,0:T(8,128)(2,1)}, u32[]{:S(2)}, u32[]{:S(2)}) async-start(bf16[64,8,768]{2,1,0:T(8,128)(2,1)} %reshape.235), calls=%async_computation.2 | async-start | bytes 1572864 | tf_op jit(solution)/shard_map/all_to_all | solution.py:115
  132.4 2.9 multiply_convert_fusion
  140.1 13.3 %all-to-all-done.2 = bf16[64,8,768]{2,1,0:T(8,128)(2,1)} async-done(((bf16[64,8,768]{2,1,0:T(8,128)(2,1)}), bf16[64,8,768]{2,1,0:T(8,128)(2,1)}, u32[]{:S(2)}, u32[]{:S(2)}) %all-to-all-start.2) | async-done | bytes 786464 | tf_op jit(solution)/shard_map/all_to_all | solution.py:115
  153.3 2.8 reshape.236
  156.1 2.3 copy.122
  159.8 2.9 fusion.54
  162.8 797.1 %all-reduce.5.cloned.1.call-done = (f32[512,1536]{1,0:T(8,128)}, f32[512,512]{1,0:T(8,128)}) async-done(((f32[512,1536]{1,0:T(8,128)}, f32[512,512]{1,0:T(8,128)}), (f32[512,1536]{1,0:T(8,128)}, f32[512,512]{1,0:T(8,128)})) %all-reduce.5.cloned.1.call-update) | async-done | bytes 4194320 | tf_op jit(solution)/shard_map/psum | solution.py:12
  960.0 3.6 fusion.34
  963.6 208.9 %psum.46 = f32[512]{0:T(512)S(1)} all-reduce(f32[512]{0:T(512)S(1)} %get-tuple-element.60), channel_id=1, replica_groups=mesh['seq'=64,'dp'=4] {'seq'}, use_global_device_ids=true, to_apply=%region_13.14 | all-reduce | flops 512 | bytes 4096 | tf_op jit(solution)/shard_map/psum | solution.py:12
  1172.5 36.5 %psum.47 = f32[512]{0:T(512)S(1)} all-reduce(f32[512]{0:T(512)S(1)} %psum.46), channel_id=1, replica_groups=mesh['seq'=64,'dp'=4] {'dp'}, use_global_device_ids=true, to_apply=%region_14.15 | all-reduce | flops 512 | bytes 4096 | tf_op jit(solution)/shard_map/psum | solution.py:13
  1209.5 2.4 fusion.40
  (75 shorter events, 31.0 us)
Async XLA Ops:
  7.2 1.0 copy-start
  7.2 19.7 %copy-start.1 = (bf16[1,1,512,512]{3,2,1,0:T(8,128)(2,1)S(1)}, bf16[1,1,512,512]{3,2,1,0:T(8,128)(2,1)}, u32[]{:S(2)}) copy-start(bf16[1,1,512,512]{3,2,1,0:T(8,128)(2,1)} %param.5) | copy-start | bytes 1572868
  9.7 0.8 copy-start.3
  14.6 26.0 %all-to-all-start.1 = ((bf16[64,2,1024]{2,1,0:T(2,128)(2,1)}), bf16[64,2,1024]{2,1,0:T(2,128)(2,1)}, u32[]{:S(2)}, u32[]{:S(2)}) async-start(bf16[64,2,1024]{2,1,0:T(2,128)(2,1)} %reshape.245), calls=%async_computation.1 | async-start | bytes 524288 | tf_op jit(solution)/shard_map/all_to_all | solution.py:109
  28.8 1.0 copy-start.16
  37.1 14.1 %copy-start.14 = (bf16[512,3,4,64]{0,3,2,1:T(8,128)(2,1)S(1)}, bf16[512,3,4,64]{0,3,2,1:T(8,128)(2,1)}, u32[]{:S(2)}) copy-start(bf16[512,3,4,64]{0,3,2,1:T(8,128)(2,1)} %get-tuple-element.76) | copy-start | bytes 2359300
  40.5 32.7 %all-to-all-start = ((bf16[64,2,3072]{2,1,0:T(2,128)(2,1)}), bf16[64,2,3072]{2,1,0:T(2,128)(2,1)}, u32[]{:S(2)}, u32[]{:S(2)}) async-start(bf16[64,2,3072]{2,1,0:T(2,128)(2,1)} %reshape.247), calls=%async_computation | async-start | bytes 1572864 | tf_op jit(solution)/shard_map/all_to_all | solution.py:103
  52.2 3.7 copy-start.6
  55.9 2.8 copy-start.4
  87.6 1.8 copy-start.8
  87.6 1.8 copy-start.9
  88.1 1.3 copy-start.12
  94.7 22.8 %all-to-all-start.3 = ((bf16[64,8,256]{2,1,0:T(8,128)(2,1)}), bf16[64,8,256]{2,1,0:T(8,128)(2,1)S(1)}, u32[]{:S(2)}, u32[]{:S(2)}) async-start(bf16[64,8,256]{2,1,0:T(8,128)(2,1)} %copy.141), calls=%async_computation.3 | async-start | bytes 524288 | tf_op jit(solution)/shard_map/all_to_all | solution.py:108
  108.0 3.2 copy-start.15
  117.6 12.9 %copy-start.10 = (bf16[64,8,256]{2,1,0:T(8,128)(2,1)}, bf16[64,8,256]{2,1,0:T(8,128)(2,1)S(1)}, u32[]{:S(2)}) copy-start(bf16[64,8,256]{2,1,0:T(8,128)(2,1)S(1)} %all-to-all-done.3) | copy-start | bytes 786436
  117.6 35.8 %all-to-all-start.2 = ((bf16[64,8,768]{2,1,0:T(8,128)(2,1)}), bf16[64,8,768]{2,1,0:T(8,128)(2,1)}, u32[]{:S(2)}, u32[]{:S(2)}) async-start(bf16[64,8,768]{2,1,0:T(8,128)(2,1)} %reshape.235), calls=%async_computation.2 | async-start | bytes 1572864 | tf_op jit(solution)/shard_map/all_to_all | solution.py:115
  130.5 829.4 %all-reduce.5.cloned.1.call-start = ((), (), s32[]{:S(2)}) async-start(), calls=%async_computation.4 | async-start | bytes 8388608 | tf_op jit(solution)/shard_map/psum | solution.py:12
  130.5 1.8 copy-start.5
  130.6 1.8 copy-start.7
  135.3 2.7 copy-start.11
  136.8 1.8 copy-start.13
  136.8 1.8 copy-start.2
  162.8 1049.1 %all-reduce.7.cloned.1.call-start = ((), (), s32[]{:S(2)}) async-start(), calls=%async_computation.5 | async-start | bytes 8388608 | tf_op jit(solution)/shard_map/psum | solution.py:13
Sparse Core Ops, SparseCore 0:
  162.9 796.9 all-reduce.4
  962.7 167.4 all-reduce.6
